TPU v7x, 256 devices: a whole 4x4x8 slice. The times are simulated.
256 devices in a mesh: req: 32 (over z, x), row: 2 (over core), col: 4 (over y).
Axes of the slice: x: 4, y: 4, z: 8, core: 2. Of those that a mesh axis runs over, the one named last changes fastest.
Arguments:
- tokens: bfloat16 [32768, 1024], P(('req', 'row'), 'col'), may hold values from -6 to 6
- w_proj: bfloat16 [1024, 8, 512], P('col', 'row'), may hold values from -0.1875 to 0.1875
- adapter_a: bfloat16 [64, 1024, 16], P('req'), may hold values from -0.1875 to 0.1875
- adapter_b: bfloat16 [64, 16, 8, 256], P('req', None, 'row'), may hold values from -0.8984375 to 0.8984375
- adapter_row: int32 [64], replicated, may hold values from 0 to 63, each once
- adapter_of: int32 [32, 2], replicated, may hold values from 0 to 63
- len_blocks: int32 [32, 2], replicated, may hold values from 1 to 12, 16 in all within a row
- state_slot: int32 [64], replicated, may hold values from 0 to 63, as said below
- init_state: float32 [64, 8, 128, 128], P('req', 'row'), may hold values from -3 to 3
- decay: float32 [512, 8], P(('req', 'col'), 'row'), may hold values from 0 to 1, as said below
Outputs:
- memory_out: bfloat16 [32768, 1024], P(('req', 'col'), 'row')
Inputs may be any that keep to these rules, and one draw needn't show every extreme that they name: `len_blocks`: each row sums to 16. `state_slot`: a permutation of the slots; slots k * 2 to (k + 1) * 2 - 1 are those of req index k. The 2 requests of req index g take one slot of req index (g - 1) mod 32 and one of req index (g - 16) mod 32, in an order and at positions within those indices that vary by draw. `decay`: every factor is above 0 and at most 1.
All inputs are finite; a program needn't handle non-finite values.
Results may differ from a plain program's by a relative error of at most 0.0062.
Values may be sent and summed in bfloat16 or wider, within the bound.
A program may use at most 128 MiB of HBM per device.

v0:
```python
import math
import jax
import jax.numpy as jnp
from jax import lax
from jax.sharding import PartitionSpec as P

BLK = 64


def carried_in(value, axis, join, neutral):
    place = lax.axis_index(axis)
    gathered = jax.tree.map(
        lambda a, kind: lax.all_gather(a.astype(kind), axis),
        value,
        jax.tree.map(lambda a: jnp.bfloat16 if a.dtype == jnp.float32 else a.dtype, value),
    )
    state = jax.tree.map(lambda a, e: jnp.zeros_like(a) + jnp.asarray(e, a.dtype), value, neutral)

    def one(lap, state):
        return join(
            state,
            jax.tree.map(
                lambda a, own: lax.dynamic_index_in_dim(a, lap, 0, False).astype(own.dtype),
                gathered,
                value,
            ),
        )

    return lax.fori_loop(0, place, one, state)


def unit(values):
    scale = lax.rsqrt(jnp.mean(values * values, axis=-1, keepdims=True) + 1e-06)
    return values * scale / math.sqrt(values.shape[-1])


def block_info(lengths, block_ids):
    starts = jnp.cumsum(lengths) - lengths
    is_start = jnp.any(block_ids[:, None] == starts[None, :], axis=1)
    request = jnp.sum((block_ids[:, None] >= starts[None, :]).astype(jnp.int32), axis=1) - 1
    return (is_start, request)


def add_adapter(base_part, delta):
    return jnp.stack(
        [
            base_part[:, :, 0] + delta[:, :, 0],
            base_part[:, :, 1],
            base_part[:, :, 2] + delta[:, :, 1],
            base_part[:, :, 3],
        ],
        axis=2,
    )


def compose(earlier, later):
    return (earlier[0] * later[0], later[0][:, None, None] * earlier[1] + later[1])


def body(
    tokens,
    w_proj,
    adapter_a,
    adapter_b,
    adapter_row,
    adapter_of,
    len_blocks,
    state_slot,
    init_state,
    decay,
):
    highest = lax.Precision.HIGHEST
    group_id = lax.axis_index("req")
    column = lax.axis_index("col")
    n_col = lax.axis_size("col")
    width = adapter_a.shape[1]
    rank = adapter_a.shape[2]
    req_grp = adapter_of.shape[1]
    heads_here = w_proj.shape[1]
    head_dim = w_proj.shape[2] // 4
    slice_width = tokens.shape[1]
    gathered = lax.all_gather(tokens, "row", axis=0, tiled=True)
    group_tok = gathered.shape[0]
    own_count = group_tok // n_col
    nblk_group = group_tok // BLK
    nblk_here = own_count // BLK
    block_ids = jnp.arange(nblk_group, dtype=jnp.int32)
    is_start, request = block_info(len_blocks[group_id], block_ids)
    onehot = (
        jnp.repeat(request, BLK)[:, None] == jnp.arange(req_grp, dtype=jnp.int32)[None, :]
    ).astype(jnp.float32)
    picked = adapter_row[adapter_of[group_id]]
    table_a, table_b = (
        lax.all_gather(adapter_a, "req", axis=0, tiled=True),
        lax.all_gather(adapter_b, "req", axis=0, tiled=True),
    )
    chosen_a = table_a[picked]
    chosen_b = table_b[picked]
    a_stack = jnp.transpose(chosen_a, (1, 0, 2)).reshape(width, req_grp * rank)
    b_stack = chosen_b.reshape(req_grp * rank, heads_here * 2 * head_dim).astype(jnp.float32)
    w_flat = w_proj.reshape(w_proj.shape[0], heads_here * 4 * head_dim)
    a_part = lax.dynamic_slice_in_dim(a_stack, column * slice_width, slice_width, 0)
    count = own_count * lax.axis_size("col")
    projected = jnp.dot(gathered, w_flat, preferred_element_type=jnp.float32)
    lowrank = jnp.dot(gathered, a_part, preferred_element_type=jnp.float32).reshape(
        count, req_grp, rank
    )
    lowrank = (lowrank * onehot[:, :, None]).reshape(count, req_grp * rank)
    delta = jnp.dot(lowrank, b_stack, precision=highest)
    joined = add_adapter(
        projected.reshape(count, heads_here, 4, head_dim),
        delta.reshape(count, heads_here, 2, head_dim),
    )
    summed = lax.psum_scatter(
        joined.reshape(count, heads_here * 4 * head_dim), "col", scatter_dimension=0, tiled=True
    )
    parts = summed.reshape(own_count, heads_here, 4, head_dim).astype(jnp.bfloat16)
    here_start = lax.dynamic_slice_in_dim(is_start, column * nblk_here, nblk_here, 0)
    here_request = lax.dynamic_slice_in_dim(request, column * nblk_here, nblk_here, 0)
    state_table = lax.all_gather(init_state, "req", axis=0, tiled=True)
    state_index = state_slot[group_id * req_grp + here_request]
    query = unit(parts[:, :, 0].astype(jnp.float32)).reshape(nblk_here, BLK, heads_here, head_dim)
    keys_n = unit(parts[:, :, 1].astype(jnp.float32)).reshape(nblk_here, BLK, heads_here, head_dim)
    values = parts[:, :, 2].astype(jnp.float32).reshape(nblk_here, BLK, heads_here, head_dim)
    causal = jnp.tril(jnp.ones((BLK, BLK), jnp.float32))

    def step(carry, blocks):
        amount, state = carry
        q_block, k_block, v_block, fade, start_here, slot = blocks
        amount = jnp.where(start_here, jnp.zeros_like(amount), amount)
        state = jnp.where(start_here, state_table[slot], state)
        read = jnp.einsum("thd,hde->the", q_block, state, precision=highest)
        scores = jnp.einsum("thd,shd->hts", q_block, k_block, precision=highest) * causal[None]
        inner = jnp.einsum("hts,she->the", scores, v_block, precision=highest)
        update = jnp.einsum("thd,the->hde", k_block, v_block, precision=highest) / BLK
        return ((fade * amount, fade[:, None, None] * state + update), (read + inner, amount))

    start_carry = (
        jnp.ones((heads_here,), jnp.float32),
        jnp.zeros((heads_here, head_dim, head_dim), jnp.float32),
    )
    last_carry, (local_mem, amounts) = lax.scan(
        step, start_carry, (query, keys_n, values, decay, here_start, state_index)
    )
    identity = (
        jnp.ones((heads_here,), jnp.float32),
        jnp.zeros((heads_here, head_dim, head_dim), jnp.float32),
    )
    incoming = carried_in(last_carry, "col", compose, identity)
    carried = jnp.einsum("nthd,hde->nthe", query, incoming[1], precision=highest)
    mem = local_mem + carried * amounts[:, None, :, None]
    gate_part = parts[:, :, 3].astype(jnp.float32)
    result = jax.nn.sigmoid(gate_part) * mem.reshape(own_count, heads_here, head_dim)
    return result.reshape(own_count, heads_here * head_dim).astype(jnp.bfloat16)


def solution(mesh):
    placed = (
        P(("req", "row"), "col"),
        P("col", "row", None),
        P("req", None, None),
        P("req", None, "row", None),
        P(),
        P(),
        P(),
        P(),
        P("req", "row", None, None),
        P(("req", "col"), "row"),
    )
    return jax.shard_map(
        body, mesh=mesh, in_specs=placed, out_specs=P(("req", "col"), "row"), check_vma=False
    )
```

profile of v0, /device:TPU:2, one launch (start us, length us, event | category | flops | bytes accessed | tf_op | source)
XLA Modules:
  0.0 471.5 jit_solution(1949894486857903738)
XLA Ops:
  10.1 1.5 copy.92
  12.9 2.2 all_gather.24
  15.1 4.5 fusion.29
  19.6 70.0 %all-gather.8.cloned.1.call-done = bf16[64,16,4,256]{3,1,2,0:T(8,128)(2,1)} async-done(((bf16[2,16,4,256]{3,1,2,0:T(8,128)(2,1)}), bf16[64,16,4,256]{3,1,2,0:T(8,128)(2,1)}) %all-gather.8.cloned.1.call-update) | async-done | bytes 2097168 | tf_op jit(solution)/shard_map/all_gather | solution.py:95
  89.6 2.1 gather_fusion.2
  91.8 75.5 %all-gather.6.cloned.1.call-done = bf16[64,1024,16]{1,2,0:T(8,128)(2,1)} async-done(((bf16[2,1024,16]{1,2,0:T(8,128)(2,1)}), bf16[64,1024,16]{1,2,0:T(8,128)(2,1)}) %all-gather.6.cloned.1.call-update) | async-done | bytes 2097168 | tf_op jit(solution)/shard_map/all_gather | solution.py:94
  167.3 2.1 gather_fusion.1
  169.7 1.9 fusion.32
  171.6 5.0 %slice_add_fusion.1 = (f32[1024,4,1,128]{0,3,2,1:T(8,128)S(1)}, f32[1024,4,1,128]{0,3,2,1:T(8,128)S(1)}, f32[1024,4,1,128]{0,3,2,1:T(8,128)S(1)}, f32[1024,4,1,128]{0,3,2,1:T(8,128)S(1)}) fusion(f32[1024,4,2,128]{0,3,2,1:T(8,128)S(1)} %fusion.32, f32[1024,4,4,128]{0,3,2,1:T(8,128)} %fusion.29), kind=kLoop, calls=%fused_computation.42 | loop fusion | flops 1048576 | bytes 20971520 | tf_op jit(solution)/shard_map/add | solution.py:47
  176.7 3.6 pad_maximum_fusion
  183.0 79.0 %reduce-scatter.2.cloned.1.call-done = f32[256,2048]{0,1:T(8,128)} async-done(((f32[1024,2048]{0,1:T(8,128)}), f32[256,2048]{0,1:T(8,128)}) %reduce-scatter.2.cloned.1.call-update) | async-done | bytes 2097168 | tf_op jit(solution)/shard_map/reduce_scatter | solution.py:114
  262.0 1.7 convert_element_type.78
  265.3 137.4 %all-gather.10.cloned.1.call-done = f32[64,4,128,128]{3,2,1,0:T(8,128)} async-done(((f32[2,4,128,128]{3,2,1,0:T(8,128)}), f32[64,4,128,128]{3,2,1,0:T(8,128)}) %all-gather.10.cloned.1.call-update) | async-done | bytes 16777232 | tf_op jit(solution)/shard_map/all_gather | solution.py:120
  402.6 35.4 %while.30 = (s32[]{:T(128)}, f32[4]{0:T(128)S(1)}, f32[4,128,128]{2,1,0:T(8,128)S(1)}, f32[4,64,4,128]{3,1,0,2:T(8,128)S(1)}, f32[4,4]{1,0:T(4,128)S(1)}, /*inde...) while((s32[]{:T(128)}, f32[4]{0:T(128)S(1)}, ...), condition=%wide.region_7.8_spmd.clone, body=%wide.region_6.7_spmd.clone.sunk | while | flops 151511056 | bytes 2741074 | solution.py:142
  406.1 1.9 fusion.70
  409.3 2.1 fusion.67
  415.0 1.9 fusion.70
  418.1 2.1 fusion.67
  423.8 1.9 fusion.70
  427.0 2.1 fusion.67
  432.7 1.9 fusion.70
  435.8 2.1 fusion.67
  438.3 13.3 %all-gather.1 = bf16[16,128,128]{2,1,0:T(8,128)(2,1)S(1)} all-gather(bf16[4,128,128]{2,1,0:T(8,128)(2,1)S(1)} %convert_element_type.90), channel_id=3, replica_groups=mesh['req'=32,'row'=2,'col'=4] {'col'}, dimensions={0}, use_global_device_ids=true | all-gather | bytes 655360 | tf_op jit(solution)/shard_map/all_gather | solution.py:13
  451.6 10.4 %all-reduce = bf16[16]{0:T(256)(128)(2,1)S(1)} all-reduce(bf16[16]{0:T(256)(128)(2,1)S(1)} %dynamic-update-slice), channel_id=2, replica_groups=mesh['req'=32,'row'=2,'col'=4] {'col'}, use_global_device_ids=true, to_apply=%add | all-reduce | flops 16 | bytes 64
  (101 shorter events, 24.2 us)
Async XLA Ops:
  6.5 174.6 %copy-start = (s32[64]{0:T(128)S(1)}, s32[64]{0:T(128)}, u32[]{:S(2)}) copy-start(s32[64]{0:T(128)} %param.21) | copy-start | bytes 772
  6.5 83.0 %all-gather.8.cloned.1.call-start = ((), (), s32[]{:S(2)}) async-start(), calls=%async_computation.2 | async-start | bytes 2162688 | tf_op jit(solution)/shard_map/all_gather | solution.py:95
  8.1 159.3 %all-gather.6.cloned.1.call-start = ((), (), s32[]{:S(2)}) async-start(), calls=%async_computation.1 | async-start | bytes 2162688 | tf_op jit(solution)/shard_map/all_gather | solution.py:94
  8.8 253.2 %reduce-scatter.2.cloned.1.call-start = ((), (), s32[]{:S(2)}) async-start(), calls=%async_computation.3 | async-start | bytes 10485760 | tf_op jit(solution)/shard_map/reduce_scatter | solution.py:114
  10.1 2.1 copy-start.1
  10.1 2.8 copy-start.3
  180.2 1.5 copy-start.4
  180.3 222.4 %all-gather.10.cloned.1.call-start = ((), (), s32[]{:S(2)}) async-start(), calls=%async_computation.4 | async-start | bytes 17301504 | tf_op jit(solution)/shard_map/all_gather | solution.py:120
  264.4 138.3 %copy-start.2 = (f32[4,64,4,128]{3,1,0,2:T(8,128)S(1)}, f32[4,64,4,128]{3,1,0,2:T(8,128)}, u32[]{:S(2)}) copy-start(f32[4,64,4,128]{3,1,0,2:T(8,128)} %custom-call.10) | copy-start | bytes 1572868
Sparse Core Ops, SparseCore 0:
  9.9 79.6 all-gather.7
  92.1 75.1 all-gather.5
  180.4 81.5 reduce-scatter.1
  264.4 138.1 all-gather.9
where the time goes:
time: 472 us
  waiting for transfers between devices  363 us (77%)
  blocking collectives  25.9 us (5%)
  matrix products  25.8 us (5%)
  local copies, waits for them, and re-layouts  18.8 us (4%)
  other arithmetic  16.8 us (4%)
  between operations  14 us (3%)
  loops' own time  6.94 us (1%)
    all_gather x1, waiting for transfers between devices, body(): state_table = lax.all_gather(init_state, 'req', axis=0, tiled=True)  137 us
    reduce_scatter x1, waiting for transfers between devices, body(): lax.psum_scatter(joined.reshape(count, heads_here * 4 * head_dim), 'col',...  79 us
    all_gather x1, waiting for transfers between devices, body(): lax.all_gather(adapter_a, 'req', axis=0, tiled=True)  75.5 us
    all_gather x1, waiting for transfers between devices, body(): lax.all_gather(adapter_b, 'req', axis=0, tiled=True)  70 us
    all_gather x1, blocking collectives, carried_in(): lax.all_gather(a.astype(kind), axis)  13.3 us
    unnamed x1, blocking collectives  10.4 us
  transfers between devices with their start and end apart: 4, of which 4 were waited for; matrix products, arithmetic and copies ran while one was open for 3% of the time, Pallas kernels for 0%

commit v1 on v0

--- a/solution.py
+++ b/solution.py
@@ -117,7 +117,9 @@
     parts = summed.reshape(own_count, heads_here, 4, head_dim).astype(jnp.bfloat16)
     here_start = lax.dynamic_slice_in_dim(is_start, column * nblk_here, nblk_here, 0)
     here_request = lax.dynamic_slice_in_dim(request, column * nblk_here, nblk_here, 0)
-    state_table = lax.all_gather(init_state, "req", axis=0, tiled=True)
+    state_table = jnp.concatenate(
+        lax.all_to_all(jnp.stack([init_state] * lax.axis_size("req")), "req", 0, 0), axis=0
+    )
     state_index = state_slot[group_id * req_grp + here_request]
     query = unit(parts[:, :, 0].astype(jnp.float32)).reshape(nblk_here, BLK, heads_here, head_dim)
     keys_n = unit(parts[:, :, 1].astype(jnp.float32)).reshape(nblk_here, BLK, heads_here, head_dim)

time: 472 us -> 631 us (1.34)
  waiting for transfers between devices: 363 us -> 502 us
  starting transfers between devices: 0.12 us -> 11.9 us
  local copies, waits for them, and re-layouts: 18.8 us -> 25.7 us
    all_gather x1, waiting for transfers between devices: 75.5 us -> 230 us  [body(): lax.all_gather(adapter_a, 'req', axis=0, tiled=True)]
    all_gather x1 -> x0, waiting for transfers between devices: 137 us -> none  [body(): state_table = lax.all_gather(init_state, 'req', axis=0, tiled=True)]
    all_gather x1, waiting for transfers between devices: 70 us -> 187 us  [body(): lax.all_gather(adapter_b, 'req', axis=0, tiled=True)]
    all_to_all x0 -> x1, starting transfers between devices: none -> 11.8 us  [body(): lax.all_to_all(jnp.stack([init_state] * lax.axis_size('req')), 'req', 0, 0)]
    another operation x1 -> x2, local copies, waits for them, and re-layouts: 0.02 us -> 8.93 us  [the longest x1 8.91 us: body(): jnp.stack([init_state] * lax.axis_size('req'))]
  transfers between devices with their start and end apart: 4 -> 4, of which waited for: 4 -> 3; matrix products, arithmetic and copies ran while one was open for 3% -> 4% of each run, Pallas kernels for 0% -> 0%
where the time goes in v1:
time: 631 us; the launch traced here: 630 us
  waiting for transfers between devices  502 us (80%)
  matrix products  26.8 us (4%)
  local copies, waits for them, and re-layouts  25.7 us (4%)
  blocking collectives  23.5 us (4%)
  other arithmetic  17.3 us (3%)
  between operations  14 us (2%)
  starting transfers between devices  11.9 us (2%)
  loops' own time  8.46 us (1%)
    all_gather x1, waiting for transfers between devices, body(): lax.all_gather(adapter_a, 'req', axis=0, tiled=True)  230 us
    all_gather x1, waiting for transfers between devices, body(): lax.all_gather(adapter_b, 'req', axis=0, tiled=True)  187 us
    reduce_scatter x1, waiting for transfers between devices, body(): lax.psum_scatter(joined.reshape(count, heads_here * 4 * head_dim), 'col',...  84.8 us
    all_gather x1, blocking collectives, carried_in(): lax.all_gather(a.astype(kind), axis)  13.4 us
  transfers between devices with their start and end apart: 4, of which 3 were waited for; matrix products, arithmetic and copies ran while one was open for 4% of the time, Pallas kernels for 0%

profile of v1, /device:TPU:2, one launch (start us, length us, event | category | flops | bytes accessed | tf_op | source)
XLA Modules:
  0.0 629.5 jit_solution(12986283949152098226)
XLA Ops:
  6.5 8.9 %stack.5 = f32[32,2,4,128,128]{4,3,2,1,0:T(8,128)} broadcast(f32[2,4,128,128]{3,2,1,0:T(8,128)} %param.22), dimensions={1,2,3,4} | broadcast | bytes 17301504 | tf_op jit(solution)/shard_map/stack | solution.py:121
  15.5 11.8 %all-to-all-start = ((f32[32,2,4,128,128]{4,3,2,1,0:T(8,128)}), f32[32,2,4,128,128]{4,3,2,1,0:T(8,128)}, u32[]{:S(2)}, u32[]{:S(2)}) async-start(f32[32,2,4,128,128]{4,3,2,1,0:T(8,128)} %stack.5), calls=%async_computation.1 | async-start | bytes 33554432 | tf_op jit(solution)/shard_map/all_to_all | solution.py:121
  30.9 2.2 all_gather.21
  33.1 4.5 fusion.29
  37.6 186.7 %all-gather.7.cloned.1.call-done = bf16[64,16,4,256]{3,1,2,0:T(8,128)(2,1)} async-done(((bf16[2,16,4,256]{3,1,2,0:T(8,128)(2,1)}), bf16[64,16,4,256]{3,1,2,0:T(8,128)(2,1)}) %all-gather.7.cloned.1.call-update) | async-done | bytes 2097168 | tf_op jit(solution)/shard_map/all_gather | solution.py:95
  224.3 2.1 gather_fusion.2
  226.5 229.7 %all-gather.5.cloned.1.call-done = bf16[64,1024,16]{1,2,0:T(8,128)(2,1)} async-done(((bf16[2,1024,16]{1,2,0:T(8,128)(2,1)}), bf16[64,1024,16]{1,2,0:T(8,128)(2,1)}) %all-gather.5.cloned.1.call-update) | async-done | bytes 2097168 | tf_op jit(solution)/shard_map/all_gather | solution.py:94
  456.2 2.1 gather_fusion.1
  458.6 1.9 fusion.32
  460.5 5.0 slice_add_fusion.1
  465.6 3.5 pad_maximum_fusion
  471.2 84.8 %reduce-scatter.2.cloned.1.call-done = f32[256,2048]{0,1:T(8,128)} async-done(((f32[1024,2048]{0,1:T(8,128)}), f32[256,2048]{0,1:T(8,128)}) %reduce-scatter.2.cloned.1.call-update) | async-done | bytes 2097168 | tf_op jit(solution)/shard_map/reduce_scatter | solution.py:114
  556.0 1.7 convert_element_type.78
  559.4 39.1 %while.30 = (s32[]{:T(128)}, f32[4]{0:T(128)S(1)}, f32[4,128,128]{2,1,0:T(8,128)S(1)}, f32[4,64,4,128]{3,1,0,2:T(8,128)S(1)}, f32[4,4]{1,0:T(4,128)S(1)}, /*inde...) while((s32[]{:T(128)}, f32[4]{0:T(128)S(1)}, ...), condition=%wide.region_7.8_spmd.clone, body=%wide.region_6.7_spmd.clone.sunk | while | flops 151511056 | bytes 2741074 | solution.py:144
  563.4 2.0 fusion.70
  566.8 2.3 fusion.67
  573.2 2.0 fusion.70
  576.6 2.3 fusion.67
  583.0 2.0 fusion.70
  586.4 2.3 fusion.67
  592.8 2.0 fusion.70
  596.2 2.3 fusion.67
  598.8 13.4 %all-gather.1 = bf16[16,128,128]{2,1,0:T(8,128)(2,1)S(1)} all-gather(bf16[4,128,128]{2,1,0:T(8,128)(2,1)S(1)} %convert_element_type.90), channel_id=3, replica_groups=mesh['req'=32,'row'=2,'col'=4] {'col'}, dimensions={0}, use_global_device_ids=true | all-gather | bytes 655360 | tf_op jit(solution)/shard_map/all_gather | solution.py:13
  612.2 7.9 %all-reduce = bf16[16]{0:T(256)(128)(2,1)S(1)} all-reduce(bf16[16]{0:T(256)(128)(2,1)S(1)} %dynamic-update-slice), channel_id=2, replica_groups=mesh['req'=32,'row'=2,'col'=4] {'col'}, use_global_device_ids=true, to_apply=%add | all-reduce | flops 16 | bytes 64
  (109 shorter events, 23.7 us)
Async XLA Ops:
  6.5 462.9 %copy-start = (s32[64]{0:T(128)S(1)}, s32[64]{0:T(128)}, u32[]{:S(2)}) copy-start(s32[64]{0:T(128)} %param.21) | copy-start | bytes 772
  15.4 11.9 %copy-start.5 = (bf16[2,16,4,256]{3,2,1,0:T(4,128)(2,1)S(1)}, bf16[2,16,4,256]{3,2,1,0:T(4,128)(2,1)}, u32[]{:S(2)}) copy-start(bf16[2,16,4,256]{3,2,1,0:T(4,128)(2,1)} %param.17) | copy-start | bytes 196612
  15.5 13.4 %copy-start.6 = (s32[32,2]{0,1:T(2,128)S(1)}, s32[32,2]{0,1:T(2,128)}, u32[]{:S(2)}) copy-start(s32[32,2]{0,1:T(2,128)} %param.19) | copy-start | bytes 772
  15.5 13.4 %copy-start.7 = (s32[32,2]{0,1:T(2,128)S(1)}, s32[32,2]{0,1:T(2,128)}, u32[]{:S(2)}) copy-start(s32[32,2]{0,1:T(2,128)} %param.20) | copy-start | bytes 772
  15.5 14.0 %copy-start.2 = (bf16[256,4,512]{2,1,0:T(4,128)(2,1)S(1)}, bf16[256,4,512]{2,1,0:T(4,128)(2,1)}, u32[]{:S(2)}) copy-start(bf16[256,4,512]{2,1,0:T(4,128)(2,1)} %param.15) | copy-start | bytes 3145732
  15.5 543.8 %all-to-all-start = ((f32[32,2,4,128,128]{4,3,2,1,0:T(8,128)}), f32[32,2,4,128,128]{4,3,2,1,0:T(8,128)}, u32[]{:S(2)}, u32[]{:S(2)}) async-start(f32[32,2,4,128,128]{4,3,2,1,0:T(8,128)} %stack.5), calls=%async_computation.1 | async-start | bytes 33554432 | tf_op jit(solution)/shard_map/all_to_all | solution.py:121
  27.3 197.0 %all-gather.7.cloned.1.call-start = ((), (), s32[]{:S(2)}) async-start(), calls=%async_computation.3 | async-start | bytes 2162688 | tf_op jit(solution)/shard_map/all_gather | solution.py:95
  28.0 428.2 %all-gather.5.cloned.1.call-start = ((), (), s32[]{:S(2)}) async-start(), calls=%async_computation.2 | async-start | bytes 2162688 | tf_op jit(solution)/shard_map/all_gather | solution.py:94
  28.8 527.2 %reduce-scatter.2.cloned.1.call-start = ((), (), s32[]{:S(2)}) async-start(), calls=%async_computation.4 | async-start | bytes 10485760 | tf_op jit(solution)/shard_map/reduce_scatter | solution.py:114
  29.4 0.8 copy-start.1
  29.4 1.5 copy-start.4
  469.1 1.0 copy-start.8
  558.4 1.0 copy-start.3
Sparse Core Ops, SparseCore 0:
  30.7 193.5 all-gather.6
  226.9 229.3 all-gather.4
  469.2 86.6 reduce-scatter.1
